TPU v7x, 32 devices: a whole 2x2x4 slice. The times are simulated.
32 devices in a mesh: groups: 2 (over y), lib: 4 (over z), tmpl: 2 (over x), sub: 2 (over core).
Axes of the slice: x: 2, y: 2, z: 4, core: 2. Of those that a mesh axis runs over, the one named last changes fastest.
Arguments:
- coords: float32 [512, 3, 128], P(('groups', 'lib', 'tmpl')), parts along dimension 0, may hold values from -5 to 5
- atom_type: int32 [512, 128], P(('groups', 'lib', 'tmpl')), parts along dimension 0, may hold values from 0 to 15
- channel: int32 [512, 128], P(('groups', 'lib', 'tmpl')), parts along dimension 0, may hold values from 0 to 2
- charge: float32 [512, 128], P(('groups', 'lib', 'tmpl')), parts along dimension 0, may hold values from -3 to 3
- pair_owner: int32 [512, 4], P(('groups', 'lib', 'tmpl')), parts along dimension 0, may hold values from 0 to 7, all different within a row; in each aligned block of 32 rows (0 to 31, 32 to 63, ...) at most 32 rows name the same one
- pair_slot: int32 [512, 4], P(('groups', 'lib', 'tmpl')), parts along dimension 0, may hold values from 0 to 511
- type_table: float32 [16, 2], replicated, may hold values from 0.3 to 3
- widths: float32 [5], replicated, may hold values from 0.3 to 1.2
- tmpl_points: float32 [4096, 3, 256], P(('lib', 'tmpl'), None, 'sub'), may hold values from -5 to 5
- tmpl_weights: bfloat16 [4096, 5, 256], P(('lib', 'tmpl'), None, 'sub'), may hold values from -3 to 3
Outputs:
- scores: float32 [512, 4], P(('groups', 'lib', 'tmpl')), parts along dimension 0
- pose_grad: float32 [512, 12], P(('groups', 'lib', 'tmpl')), parts along dimension 0
- weight_grad: float32 [8192, 5, 256], P(('groups', 'lib', 'tmpl'), None, 'sub'), parts along dimension 0
There are 2 independent parts, one for each index of `groups`. A program takes and returns all parts, laid end to end along the dimension named above; an argument that names none is the same for every part. Nothing has to cross between parts.
Inputs may be any that keep to these rules, and one draw needn't show every extreme that they name: `pair_owner`: each row names 4 different owners; among the 32 rows of one device (aligned blocks) no owner is named more than 32 times, a bound that some block reaches.
All inputs are finite; a program needn't handle non-finite values.
Results may differ from a plain program's by a relative error of at most 0.0003.
Values sent between devices are 32-bit elements; how exact they have to be, the bound alone decides.
A program may use at most 64 MiB of HBM per device.

v0:
```python
import functools
import math

import jax
import jax.numpy as jnp
from jax import lax
from jax.experimental import pallas as pl
from jax.experimental.pallas import tpu as pltpu
from jax.sharding import PartitionSpec as P

MESH = pl.DeviceIdType.MESH
F32 = jnp.float32
BF16 = jnp.bfloat16
GROUP = 32
FLIP = True
FLAGS = {}
SKEW = 2
VALUES = 16


def gather_kernel(libs, tmpls, xyz_ref, charge_ref, type_ref, chan_ref, owner_ref, slot_ref, real_ref, whole_ref, name_ref,
                  local_sem, z_send, z_recv, x_send, x_recv, s_send, s_recv):
    l = lax.axis_index("lib")
    t = lax.axis_index("tmpl")
    s = lax.axis_index("sub")
    half = real_ref.shape[3] // 2
    moves = [(xyz_ref, real_ref.at[l, t, pl.ds(0, 3)]), (charge_ref, real_ref.at[l, t, 3]), (type_ref, whole_ref.at[l, t, 0]),
             (chan_ref, whole_ref.at[l, t, 1]), (owner_ref, name_ref.at[l, t, 0]), (slot_ref, name_ref.at[l, t, 1])]
    moves = [pltpu.make_async_copy(src, dst, local_sem.at[n]) for n, (src, dst) in enumerate(moves)]
    for move in moves:
        move.start()
    barrier = pltpu.get_barrier_semaphore()

    @pl.loop(1, libs)
    def _(k):
        pl.semaphore_signal(barrier, inc=1, device_id={"lib": lax.rem(l + k, libs)}, device_id_type=MESH)

    @pl.loop(1, tmpls)
    def _(k):
        pl.semaphore_signal(barrier, inc=1, device_id={"tmpl": lax.rem(t + k, tmpls)}, device_id_type=MESH)

    pl.semaphore_signal(barrier, inc=1, device_id={"sub": 1 - s}, device_id_type=MESH)
    for move in moves:
        move.wait()
    pl.semaphore_wait(barrier, libs + tmpls - 1)

    def chunk(k, m):
        at = (lax.rem(l - k + libs, libs), lax.rem(t - m + tmpls, tmpls))
        part = pl.ds(s * half, half)
        return real_ref.at[at + (slice(None), part)], whole_ref.at[at + (slice(None), part)], name_ref.at[at + (s,)]

    class Bundle:
        def __init__(self, refs, send, recv, device):
            self.copies = [pltpu.make_async_remote_copy(
                src_ref=ref, dst_ref=ref, send_sem=send(n), recv_sem=recv(n), device_id=device, device_id_type=MESH)
                for n, ref in enumerate(refs)]

        def start(self):
            for c in self.copies:
                c.start()

        def wait_recv(self):
            for c in self.copies:
                c.wait_recv()

        def wait_send(self):
            for c in self.copies:
                c.wait_send()

    def z_copy(k):
        return Bundle(chunk(0, 0), lambda n: z_send.at[k, n], lambda n: z_recv.at[k, n], {"lib": lax.rem(l + k, libs)})

    def x_copy(k, m):
        return Bundle(chunk(k, 0), lambda n: x_send.at[k, m, n], lambda n: x_recv.at[k, m, n], {"tmpl": lax.rem(t + m, tmpls)})

    def s_copy(k, m):
        return Bundle(chunk(k, m), lambda n: s_send.at[k, m, n], lambda n: s_recv.at[k, m, n], {"sub": 1 - s})

    @pl.loop(1, tmpls)
    def _(m):
        x_copy(0, m).start()

    @pl.loop(1, libs)
    def _(k):
        z_copy(k).start()

    @pl.loop(1, libs)
    def _(k):
        z_copy(k).wait_recv()

        @pl.loop(1, tmpls)
        def _(m):
            x_copy(k, m).start()

        s_copy(k, 0).start()

    @pl.loop(1, tmpls)
    def _(m):
        @pl.loop(0, libs)
        def _(k):
            x_copy(k, m).wait_recv()
            s_copy(k, m).start()

    @pl.loop(1, libs)
    def _(k):
        z_copy(k).wait_send()
        s_copy(k, 0).wait_send()
        s_copy(k, 0).wait_recv()

    @pl.loop(1, tmpls)
    def _(m):
        @pl.loop(0, libs)
        def _(k):
            x_copy(k, m).wait_send()
            s_copy(k, m).wait_send()
            s_copy(k, m).wait_recv()


def gather_blocks(xyz, charge, types, chans, owners, slots, libs, tmpls):
    dma = pltpu.SemaphoreType.DMA
    blocks = charge.shape[0]
    lead = (libs, tmpls)
    vmem = pl.BlockSpec(memory_space=pltpu.VMEM)
    return pl.pallas_call(
        functools.partial(gather_kernel, libs, tmpls),
        out_shape=(jax.ShapeDtypeStruct(lead + (4, blocks, 128), F32), jax.ShapeDtypeStruct(lead + (2, blocks, 128), jnp.int32),
                   jax.ShapeDtypeStruct(lead + (2,) + owners.shape, jnp.int32)),
        in_specs=[pl.BlockSpec(memory_space=pl.ANY)] * 6,
        out_specs=(vmem,) * 3,
        scratch_shapes=[dma((6,)), dma((libs, 3)), dma((libs, 3)), dma(lead + (3,)), dma(lead + (3,)),
                        dma(lead + (3,)), dma(lead + (3,))],
        compiler_params=pltpu.CompilerParams(collective_id=0, has_side_effects=True, vmem_limit_bytes=60 << 20),
    )(xyz, charge, types, chans, owners, slots)


def split3(a):
    h = a.astype(BF16).astype(F32)
    r = a - h
    m = r.astype(BF16).astype(F32)
    return h, m, r - m


def split2(a):
    h = a.astype(BF16)
    return h, (a - h.astype(F32)).astype(BF16)


def pair_kernel(me, name_ref, widths_ref, table_ref, real_ref, whole_ref, points_ref, bf_weights_ref, wg_ref, out_ref, res_ref,
                atom_ref, weights_ref):
    devices, _, per_dev, _ = real_ref.shape
    place = me()
    res_ref[...] = jnp.zeros_like(res_ref)
    row = lax.broadcasted_iota(jnp.int32, (8, 128), 0)
    row16 = lax.broadcasted_iota(jnp.int32, (VALUES, 128), 0)
    lane16 = lax.broadcasted_iota(jnp.int32, (VALUES, 128), 1)
    low = row < 4
    log2e = math.log2(math.e)
    wide = [widths_ref[f] for f in range(5)]
    scale = [-log2e * w for w in wide]

    @pl.loop(0, 5)
    def _(f):
        wg_ref[f] = jnp.zeros(wg_ref.shape[1:], F32)
        weights_ref[f] = bf_weights_ref[f].astype(F32)

    @pl.loop(0, devices)
    def _(dev):
        types = whole_ref[dev, 0]
        chan = whole_ref[dev, 1]
        steric = jnp.zeros(types.shape, F32)
        strength = jnp.zeros(types.shape, F32)
        for n in range(table_ref.shape[1]):
            same = types == n
            steric = jnp.where(same, table_ref[0, n], steric)
            strength = jnp.where(same, table_ref[1, n], strength)
        atom_ref[dev, 0] = steric
        atom_ref[dev, 1] = strength
        atom_ref[dev, 2] = jnp.where(chan == 0, scale[2], jnp.where(chan == 1, scale[3], scale[4]))

    def front(dev, b, slot):
        valid = jnp.where(slot >= 0, F32(1), F32(0))
        slot = jnp.maximum(slot, 0)
        here = pl.ds(b, 1)
        there = pl.ds(slot, 1)
        x = [jnp.broadcast_to(real_ref[dev, c, here, :], (8, 128)) for c in range(3)]
        y = [jnp.broadcast_to(points_ref[c, there, :], (8, 128)) for c in range(3)]
        chan = whole_ref[dev, 1, here, :]
        steric = atom_ref[dev, 0, here, :] * valid
        charge = real_ref[dev, 3, here, :] * valid
        strength = atom_ref[dev, 1, here, :] * valid
        pharm_scale = atom_ref[dev, 2, here, :]

        def rows(first, norm_row, one_row, p):
            norm = p[0] * p[0] + p[1] * p[1] + p[2] * p[2]
            v = jnp.where(row == 0, p[0] * first, jnp.where(row == 1, p[1] * first, p[2] * first))
            return jnp.where(row < 3, v, jnp.where(row == norm_row, norm, jnp.where(row == one_row, 1.0, 0.0)))

        def atom_side(v):
            h, m, l = split3(v)
            return jnp.concatenate([h, h, h, m, m, l], axis=0).astype(BF16)

        xv = rows(1.0, 3, 4, x)
        xs = atom_side(xv)
        yh, ym, yl = split3(rows(-2.0, 4, 3, y))
        ys = jnp.concatenate([yh, ym, yl, yh, ym, yh], axis=0).astype(BF16)
        if FLIP:
            both = jnp.concatenate([xs, atom_side(xv * pharm_scale)], axis=1)
            dist = lax.dot_general(both, ys, (((0,), (0,)), ((), ())), preferred_element_type=F32)
            dist, pharm = dist[:128], dist[128:]
        else:
            dist = lax.dot_general(ys, xs, (((0,), (0,)), ((), ())), preferred_element_type=F32)
            pharm = dist * pharm_scale
        inner = jnp.where(row % 4 == 0, 1.0, jnp.where(row % 4 == 1, x[0], jnp.where(row % 4 == 2, x[1], x[2])))
        outer = jnp.concatenate([jnp.where(low, 1.0, x[0]), jnp.where(low, x[1], x[2])], axis=0)
        moments = outer * jnp.concatenate([inner, inner], axis=0)

        return there, y, chan, steric, charge, strength, dist, pharm, moments

    def middle(there, y, chan, steric, charge, strength, dist, pharm, moments):
        def contract(exps, coefs):
            hi, lo = split2(exps)
            rhs = jnp.concatenate([hi, lo], axis=0 if FLIP else 1)
            lhs = jnp.concatenate([moments * c for c in coefs], axis=0)
            lh, ll = split2(lhs)
            lhs2 = jnp.concatenate([lh, ll], axis=0)
            lhs2 = jnp.concatenate([lhs2, lhs2], axis=1)
            got = lax.dot_general(lhs2, rhs, (((1,), (0 if FLIP else 1,)), ((), ())), preferred_element_type=F32)
            n = VALUES * len(coefs)
            got = got[:n] + got[n:]
            return [got[VALUES * c:VALUES * (c + 1)] for c in range(len(coefs))]

        parts = contract(jnp.exp2(dist * scale[0]), [steric]) + contract(jnp.exp2(dist * scale[1]), [charge])
        parts += contract(jnp.exp2(pharm), [jnp.where(chan == c, strength, 0.0) for c in range(3)])
        return there, y, parts

    def back(there, y, parts):
        total = jnp.zeros((VALUES, 128), F32)
        score = jnp.zeros((1, 128), F32)
        for f in range(5):
            v = weights_ref[f, there, :]
            score = score + v * parts[f][0:1]
            total = total + (v * (-2.0 * wide[f])) * parts[f]
        base = jnp.concatenate([total[0:4]] * 4, axis=0)
        y16 = jnp.concatenate([jnp.where(low, 0.0, y[0]), jnp.where(low, y[1], y[2])], axis=0)
        final = jnp.where(row16 == 0, score, total - y16 * base)
        summed = jnp.sum(final, axis=1, keepdims=True)
        return there, [p[0:1] for p in parts], summed

    group = math.gcd(GROUP, per_dev)

    @pl.loop(0, devices)
    def _(dev):
        @pl.loop(0, per_dev // group)
        def _(g):
            slots = []
            for u in range(group):
                slot = jnp.int32(-1)
                for k in range(name_ref.shape[2]):
                    slot = jnp.where(name_ref[dev, 0, k, g * group + u] == place, name_ref[dev, 1, k, g * group + u], slot)
                slots.append(slot)
            best = slots[0]
            for v in slots[1:]:
                best = jnp.maximum(best, v)

            @pl.when(best >= 0)
            def _():
                fronts, middles, done = {}, {}, []
                for u in range(group + 2 * SKEW):
                    if u < group:
                        fronts[u] = front(dev, g * group + u, slots[u])
                    if SKEW <= u < group + SKEW:
                        middles[u - SKEW] = middle(*fronts.pop(u - SKEW))
                    if u >= 2 * SKEW:
                        done.append(back(*middles.pop(u - 2 * SKEW)))
                for there, wparts, summed in done:
                    for f, part in enumerate(wparts):
                        wg_ref[f, there, :] += part
                acc = res_ref[dev]
                for u, (there, wparts, summed) in enumerate(done):
                    acc = jnp.where(lane16 == g * group + u, summed, acc)
                res_ref[dev] = acc

    @pl.loop(0, devices)
    def _(dev):
        r = res_ref[dev]
        packed = r[0:4]
        for q in range(1, 4):
            packed = packed + pltpu.roll(r[4 * q:4 * q + 4], 32 * q, 1)
        out_ref[dev] = packed


def run_pairs(me, names, widths, table, real, whole, points, weights):
    tmpl_count = points.shape[1]
    devices, _, per_dev, _ = real.shape
    vmem = pl.BlockSpec(memory_space=pltpu.VMEM)
    smem = pl.BlockSpec(memory_space=pltpu.SMEM)
    return pl.pallas_call(
        functools.partial(pair_kernel, me),
        out_shape=(jax.ShapeDtypeStruct((5, tmpl_count, 128), F32), jax.ShapeDtypeStruct((devices, 4, 128), F32)),
        in_specs=[smem, smem, smem, vmem, vmem, vmem, vmem],
        out_specs=(vmem, vmem),
        scratch_shapes=[pltpu.VMEM((devices, VALUES, 128), F32), pltpu.VMEM((devices, 3, per_dev, 128), F32),
                        pltpu.VMEM((5, tmpl_count, 128), F32)],
        compiler_params=pltpu.CompilerParams(vmem_limit_bytes=60 << 20, flags=FLAGS),
    )(names, widths, table, real, whole, points, weights)


def return_kernel(libs, tmpls, res_ref, owner_ref, score_ref, pose_ref, got_ref, local_sem, send_sem, recv_sem):
    l = lax.axis_index("lib")
    t = lax.axis_index("tmpl")
    s = lax.axis_index("sub")
    owners = libs * tmpls
    count = 2 * owners
    me = (l * tmpls + t) * 2 + s
    barrier = pltpu.get_barrier_semaphore()

    def peer(k):
        other = lax.rem(me + k, count)
        return other // 2, {"lib": other // (2 * tmpls), "tmpl": lax.rem(other // 2, tmpls), "sub": lax.rem(other, 2)}

    @pl.loop(1, count)
    def _(k):
        pl.semaphore_signal(barrier, inc=1, device_id=peer(k)[1], device_id_type=MESH)

    local = pltpu.make_async_copy(res_ref.at[l * tmpls + t], got_ref.at[me], local_sem)
    local.start()
    pl.semaphore_wait(barrier, count - 1)

    def copy(k):
        block, where = peer(k)
        return pltpu.make_async_remote_copy(
            src_ref=res_ref.at[block], dst_ref=got_ref.at[me], send_sem=send_sem.at[k], recv_sem=recv_sem.at[k],
            device_id=where, device_id_type=MESH)

    @pl.loop(1, count)
    def _(k):
        copy(k).start()

    local.wait()

    @pl.loop(1, count)
    def _(k):
        copy(k).wait()

    owner = owner_ref[...]
    per_block, blocks = owner.shape

    def add(o, carry):
        total, scores = carry
        both = got_ref[2 * o] + got_ref[2 * o + 1]
        scores = jnp.where(owner == o, jnp.broadcast_to(both[0:1, :blocks], (per_block, blocks)), scores)
        return total + both, scores

    total, scores = lax.fori_loop(0, owners, add, (jnp.zeros((4, 128), F32), jnp.zeros((per_block, blocks), F32)))
    rows = [total] + [pltpu.roll(total, 128 - 32 * q, 1) for q in range(1, 4)]
    pose = jnp.concatenate([rows[1][0:1], rows[2][0:1], rows[3][0:1], rows[1][1:4], rows[2][1:4], rows[3][1:4]], axis=0)
    score_ref[...] = scores
    pose_ref[...] = pose[:, :blocks]


def send_back(res, owner_rows, libs, tmpls):
    per_block, blocks = owner_rows.shape
    dma = pltpu.SemaphoreType.DMA
    count = 2 * libs * tmpls
    vmem = pl.BlockSpec(memory_space=pltpu.VMEM)
    return pl.pallas_call(
        functools.partial(return_kernel, libs, tmpls),
        out_shape=(jax.ShapeDtypeStruct((per_block, blocks), F32), jax.ShapeDtypeStruct((12, blocks), F32)),
        in_specs=[vmem, vmem],
        out_specs=(vmem, vmem),
        scratch_shapes=[pltpu.VMEM((count, 4, 128), F32), dma, dma((count,)), dma((count,))],
        compiler_params=pltpu.CompilerParams(collective_id=1, has_side_effects=True),
    )(res, owner_rows)


def local(libs, tmpls, coords, atom_type, channel, charge, pair_owner, pair_slot, type_table, widths, tmpl_points,
          tmpl_weights):
    owners, slots = pair_owner.T, pair_slot.T
    real, whole, names = gather_blocks(jnp.transpose(coords, (1, 0, 2)), charge, atom_type, channel, owners, slots, libs, tmpls)
    count = libs * tmpls
    real, whole, names = [a.reshape((count,) + a.shape[2:]) for a in (real, whole, names)]

    def me():
        return lax.axis_index("lib") * tmpls + lax.axis_index("tmpl")

    weight_grad, res = run_pairs(me, names, widths, type_table.T, real, whole, jnp.transpose(tmpl_points, (1, 0, 2)),
                                 jnp.transpose(tmpl_weights, (1, 0, 2)))
    scores, pose = send_back(res, owners, libs, tmpls)
    return scores.T, pose.T, jnp.transpose(weight_grad, (1, 0, 2))


def solution(mesh):
    every = ("groups", "lib", "tmpl")
    in_specs = (P(every, None, None), P(every, None), P(every, None), P(every, None), P(every, None), P(every, None),
                P(), P(), P(("lib", "tmpl"), None, "sub"), P(("lib", "tmpl"), None, "sub"))
    out_specs = (P(every, None), P(every, None), P(every, None, "sub"))
    body = functools.partial(local, mesh.shape["lib"], mesh.shape["tmpl"])
    return jax.shard_map(body, mesh=mesh, in_specs=in_specs, out_specs=out_specs, check_vma=False)
```

profile of v0, /device:TPU:0, one launch (start us, length us, event | category | flops | bytes accessed | tf_op | source)
XLA Modules:
  0.0 52.5 jit_solution(16059227753161212326)
XLA Ops:
  0.6 17.0 %shard_map.121 = (f32[4,2,4,32,128]{4,3,2,1,0:T(8,128)}, s32[4,2,2,32,128]{4,3,2,1,0:T(8,128)}, s32[4,2,2,4,32]{4,3,2,1,0:T(4,128)}) custom-call(f32[3,32,128]{2,1,0:T(8,128)} %bitcast.16, f32[32,128]{1,0:T(8,128)} %charge_ref.1, s32[32,128]{1,0:T(8,128)} %type_ref.1, s32[32,128]{1,0:T(8,128)} %chan_ref.1, s32[4,32]{1,0:T(4,128)} %bitcast.18, s32[4,32]{1,0:T(4,128)} %bitcast.21), custom_call_target="tpu_custom_call" | custom-call | tf_op jit(solution)/shard_map/pallas_call | solution.py:124
  17.6 24.2 %shard_map.122 = (f32[5,512,128]{2,1,0:T(8,128)}, f32[8,4,128]{2,1,0:T(4,128)}) custom-call(s32[8,2,4,32]{3,2,1,0:T(4,128)} %bitcast.17, f32[5]{0:T(128)} %widths_ref.1, f32[2,16]{1,0:T(2,128)} %bitcast.23, f32[8,4,32,128]{3,2,1,0:T(8,128)} %bitcast.14, s32[8,2,32,128]{3,2,1,0:T(8,128)} %bitcast.15, f32[3,512,128]{2,1,0:T(8,128)} %bitcast.12, ...), custom_call_target="tpu_custom_call" | custom-call | tf_op jit(solution)/shard_map/pallas_call | solution.py:297
  41.9 8.1 %shard_map.123 = (f32[4,32]{1,0:T(4,128)}, f32[12,32]{1,0:T(8,128)}) custom-call(f32[8,4,128]{2,1,0:T(4,128)} %get-tuple-element.13.res_ref, s32[4,32]{1,0:T(4,128)} %bitcast.19), custom_call_target="tpu_custom_call" | custom-call | tf_op jit(solution)/shard_map/pallas_call | solution.py:366
  50.0 1.2 %copy.15 = f32[32,4]{0,1:T(4,128)} copy(f32[32,4]{0,1:T(4,128)} %bitcast.22) | data formatting | bytes 1024
  51.2 1.3 %copy.16 = f32[32,12]{0,1:T(8,128)} copy(f32[32,12]{0,1:T(8,128)} %bitcast.20) | data formatting | bytes 3072
where the time goes:
time: 52.9 us; the launch traced here: 52.5 us
  Pallas kernels  49.3 us (93%)
  local copies, waits for them, and re-layouts  2.53 us (5%)
  between operations  0.65 us (1%)
    pallas_call x1, Pallas kernels, run_pairs(): pl.pallas_call(functools.partial(pair_kernel, me), out_shape=(jax.ShapeDt...  24.2 us
    pallas_call x1, Pallas kernels, gather_blocks(): pl.pallas_call(functools.partial(gather_kernel, libs, tmpls), out_shape=(...  17 us
    pallas_call x1, Pallas kernels, send_back(): pl.pallas_call(functools.partial(return_kernel, libs, tmpls), out_shape=(...  8.1 us
    unnamed x2, local copies, waits for them, and re-layouts  2.53 us

commit v1 on v0

v1 whole, which is shorter than its diff:
```python
import functools
import math

import jax
import jax.numpy as jnp
from jax import lax
from jax.experimental import pallas as pl
from jax.experimental.pallas import tpu as pltpu
from jax.sharding import PartitionSpec as P

MESH = pl.DeviceIdType.MESH
F32 = jnp.float32
BF16 = jnp.bfloat16
ROWS = 16
MOMENTS = 10
SKEW = 2


def gather_kernel(libs, tmpls, xyz_ref, charge_ref, type_ref, chan_ref, owner_ref, slot_ref, real_ref, whole_ref, name_ref,
                  local_sem, z_send, z_recv, x_send, x_recv, s_send, s_recv):
    l = lax.axis_index("lib")
    t = lax.axis_index("tmpl")
    s = lax.axis_index("sub")
    half = real_ref.shape[3] // 2
    moves = [(xyz_ref, real_ref.at[l, t, pl.ds(0, 3)]), (charge_ref, real_ref.at[l, t, 3]), (type_ref, whole_ref.at[l, t, 0]),
             (chan_ref, whole_ref.at[l, t, 1]), (owner_ref, name_ref.at[l, t, 0]), (slot_ref, name_ref.at[l, t, 1])]
    moves = [pltpu.make_async_copy(src, dst, local_sem.at[n]) for n, (src, dst) in enumerate(moves)]
    for move in moves:
        move.start()
    barrier = pltpu.get_barrier_semaphore()

    @pl.loop(1, libs)
    def _(k):
        pl.semaphore_signal(barrier, inc=1, device_id={"lib": lax.rem(l + k, libs)}, device_id_type=MESH)

    @pl.loop(1, tmpls)
    def _(k):
        pl.semaphore_signal(barrier, inc=1, device_id={"tmpl": lax.rem(t + k, tmpls)}, device_id_type=MESH)

    pl.semaphore_signal(barrier, inc=1, device_id={"sub": 1 - s}, device_id_type=MESH)
    for move in moves:
        move.wait()
    pl.semaphore_wait(barrier, libs + tmpls - 1)

    def chunk(k, m):
        at = (lax.rem(l - k + libs, libs), lax.rem(t - m + tmpls, tmpls))
        part = pl.ds(s * half, half)
        return real_ref.at[at + (slice(None), part)], whole_ref.at[at + (slice(None), part)], name_ref.at[at + (s,)]

    class Bundle:
        def __init__(self, refs, send, recv, device):
            self.copies = [pltpu.make_async_remote_copy(
                src_ref=ref, dst_ref=ref, send_sem=send(n), recv_sem=recv(n), device_id=device, device_id_type=MESH)
                for n, ref in enumerate(refs)]

        def start(self):
            for c in self.copies:
                c.start()

        def wait_recv(self):
            for c in self.copies:
                c.wait_recv()

        def wait_send(self):
            for c in self.copies:
                c.wait_send()

    def z_copy(k):
        return Bundle(chunk(0, 0), lambda n: z_send.at[k, n], lambda n: z_recv.at[k, n], {"lib": lax.rem(l + k, libs)})

    def x_copy(k, m):
        return Bundle(chunk(k, 0), lambda n: x_send.at[k, m, n], lambda n: x_recv.at[k, m, n], {"tmpl": lax.rem(t + m, tmpls)})

    def s_copy(k, m):
        return Bundle(chunk(k, m), lambda n: s_send.at[k, m, n], lambda n: s_recv.at[k, m, n], {"sub": 1 - s})

    @pl.loop(1, tmpls)
    def _(m):
        x_copy(0, m).start()

    @pl.loop(1, libs)
    def _(k):
        z_copy(k).start()

    @pl.loop(1, libs)
    def _(k):
        z_copy(k).wait_recv()

        @pl.loop(1, tmpls)
        def _(m):
            x_copy(k, m).start()

        s_copy(k, 0).start()

    @pl.loop(1, tmpls)
    def _(m):
        @pl.loop(0, libs)
        def _(k):
            x_copy(k, m).wait_recv()
            s_copy(k, m).start()

    @pl.loop(1, libs)
    def _(k):
        z_copy(k).wait_send()
        s_copy(k, 0).wait_send()
        s_copy(k, 0).wait_recv()

    @pl.loop(1, tmpls)
    def _(m):
        @pl.loop(0, libs)
        def _(k):
            x_copy(k, m).wait_send()
            s_copy(k, m).wait_send()
            s_copy(k, m).wait_recv()


def gather_blocks(xyz, charge, types, chans, owners, slots, libs, tmpls):
    dma = pltpu.SemaphoreType.DMA
    blocks = charge.shape[0]
    lead = (libs, tmpls)
    vmem = pl.BlockSpec(memory_space=pltpu.VMEM)
    return pl.pallas_call(
        functools.partial(gather_kernel, libs, tmpls),
        out_shape=(jax.ShapeDtypeStruct(lead + (4, blocks, 128), F32), jax.ShapeDtypeStruct(lead + (2, blocks, 128), jnp.int32),
                   jax.ShapeDtypeStruct(lead + (2,) + owners.shape, jnp.int32)),
        in_specs=[pl.BlockSpec(memory_space=pl.ANY)] * 6,
        out_specs=(vmem,) * 3,
        scratch_shapes=[dma((6,)), dma((libs, 3)), dma((libs, 3)), dma(lead + (3,)), dma(lead + (3,)),
                        dma(lead + (3,)), dma(lead + (3,))],
        compiler_params=pltpu.CompilerParams(collective_id=0, has_side_effects=True, vmem_limit_bytes=60 << 20),
    )(xyz, charge, types, chans, owners, slots)


def split3(a):
    h = a.astype(BF16).astype(F32)
    r = a - h
    m = r.astype(BF16).astype(F32)
    return h, m, r - m


def split2(a):
    h = a.astype(BF16)
    return h, (a - h.astype(F32)).astype(BF16)


def slot_row(name_ref, dev, place):
    named = name_ref[dev, 0] == place
    return jnp.max(jnp.where(named, name_ref[dev, 1], -1), axis=0, keepdims=True)


class Pairs:
    def __init__(self, place, blocks, name_ref, widths_ref, table_ref, real_ref, whole_ref, points_ref, weights_ref, part_ref,
                 atom_ref, moment_ref, mask_ref, rows_ref, tmpl_ref, got_ref):
        self.place, self.blocks = place, blocks
        self.name_ref, self.widths_ref, self.table_ref = name_ref, widths_ref, table_ref
        self.real_ref, self.whole_ref, self.points_ref, self.weights_ref = real_ref, whole_ref, points_ref, weights_ref
        self.part_ref, self.atom_ref, self.moment_ref, self.mask_ref = part_ref, atom_ref, moment_ref, mask_ref
        self.rows_ref, self.tmpl_ref, self.got_ref = rows_ref, tmpl_ref, got_ref
        self.wide = [widths_ref[f] for f in range(5)]
        log2e = math.log2(math.e)
        self.scale = [-log2e * w for w in self.wide]
        self.ratio = self.wide[1] / self.wide[0]

    def plane(self, n):
        return pl.ds(n * self.blocks, self.blocks)

    def column(self, n, u, count=8):
        return pl.ds(n * self.blocks + u, count, stride=self.blocks)

    def clear(self):
        self.atom_ref[...] = jnp.zeros_like(self.atom_ref)
        self.moment_ref[...] = jnp.zeros_like(self.moment_ref)
        self.tmpl_ref[...] = jnp.zeros_like(self.tmpl_ref)

    def atoms(self, dev):
        x = [self.real_ref[dev, c] for c in range(3)]
        charge = self.real_ref[dev, 3]
        types = self.whole_ref[dev, 0]
        chan = self.whole_ref[dev, 1]
        steric = jnp.zeros(types.shape, F32)
        strength = jnp.zeros(types.shape, F32)
        for n in range(self.table_ref.shape[1]):
            same = types == n
            steric = jnp.where(same, self.table_ref[0, n], steric)
            strength = jnp.where(same, self.table_ref[1, n], strength)
        pharm = jnp.where(chan == 0, self.scale[2], jnp.where(chan == 1, self.scale[3], self.scale[4]))
        for c in range(3):
            self.mask_ref[self.plane(c)] = jnp.where(chan == c, 1.0, 0.0)
        second = [x[0] * x[0], x[0] * x[1], x[0] * x[2], x[1] * x[1], x[1] * x[2], x[2] * x[2]]
        norm = second[0] + second[3] + second[5]
        for s, scale in enumerate((self.scale[0], pharm)):
            for c, value in enumerate(x + [norm, None]):
                value = jnp.full(types.shape, scale) if value is None and s == 0 else scale if value is None else value * scale
                for p, piece in enumerate(split3(value)):
                    self.atom_ref[self.plane((3 * s + p) * 8 + c)] = piece
        for c, coef in enumerate((steric, charge, strength)):
            for k, moment in enumerate([None] + x + second):
                value = coef if moment is None else coef * moment
                high = value.astype(BF16).astype(F32)
                self.moment_ref[self.plane(2 * c * ROWS + k)] = high
                self.moment_ref[self.plane((2 * c + 1) * ROWS + k)] = value - high

    def templates(self, dev):
        slots = jnp.maximum(slot_row(self.name_ref, dev, self.place), 0)
        for u in range(self.blocks):
            there = pl.ds(slots[0, u], 1)
            for c in range(3):
                self.rows_ref[pl.ds(c * self.blocks + u, 1)] = self.points_ref[c, there, :]
            for f in range(5):
                self.rows_ref[pl.ds((3 + f) * self.blocks + u, 1)] = self.weights_ref[f, there, :]
        y = [self.rows_ref[self.plane(c)] for c in range(3)]
        norm = y[0] * y[0] + y[1] * y[1] + y[2] * y[2]
        for c, value in enumerate([-2.0 * y[0], -2.0 * y[1], -2.0 * y[2], jnp.ones_like(norm), norm]):
            for p, piece in enumerate(split3(value)):
                self.tmpl_ref[self.plane(8 * p + c)] = piece

    def front(self, u):
        def side(ref, base, order):
            pieces = [ref[self.column(base + 8 * p, u)] for p in range(3)]
            return jnp.concatenate([pieces[p] for p in order], axis=0).astype(BF16)

        xs = jnp.concatenate([side(self.atom_ref, 24 * s, (0, 0, 0, 1, 1, 2)) for s in range(2)], axis=1)
        ys = side(self.tmpl_ref, 0, (0, 1, 2, 0, 1, 0))
        return u, lax.dot_general(xs, ys, (((0,), (0,)), ((), ())), preferred_element_type=F32)

    def middle(self, u, dist):
        def side(c):
            rows = [self.moment_ref[self.column(2 * c * ROWS + 8 * r, u)] for r in range(4)]
            return jnp.concatenate(rows, axis=0).astype(BF16)

        def contract(power, lhs):
            hi, lo = split2(jnp.exp2(power))
            got = lax.dot_general(jnp.concatenate([lhs, lhs], axis=1), jnp.concatenate([hi, lo], axis=0),
                                  (((1,), (0,)), ((), ())), preferred_element_type=F32)
            return [got[r:r + ROWS] + got[r + ROWS:r + 2 * ROWS] for r in range(0, got.shape[0], 2 * ROWS)]

        strength = side(2)
        pharm = [strength * jnp.broadcast_to(self.mask_ref[pl.ds(c * self.blocks + u, 1)], strength.shape).astype(BF16)
                 for c in range(3)]
        near, far = dist[:128], dist[128:]
        return u, contract(near, side(0)) + contract(near * self.ratio, side(1)) + contract(far, jnp.concatenate(pharm, axis=0))

    def back(self, u, parts):
        for f, part in enumerate(parts):
            self.got_ref[self.column(f * ROWS, u)] = part[:8]
            self.got_ref[self.column(f * ROWS + 8, u, MOMENTS - 8)] = part[8:MOMENTS]

    def finish(self, dev):
        blocks = self.blocks
        lane = lax.broadcasted_iota(jnp.int32, (blocks, 128), 1)
        y = [self.rows_ref[self.plane(c)] for c in range(3)]
        score = jnp.zeros((blocks, 128), F32)
        total = [jnp.zeros((blocks, 128), F32)] * MOMENTS
        for f in range(5):
            v = self.rows_ref[self.plane(3 + f)]
            first = self.got_ref[self.plane(f * ROWS)]
            self.part_ref[f, pl.ds(dev * blocks, blocks)] = first
            score = score + v * first
            v = v * (-2.0 * self.wide[f])
            total = [t + v * (first if k == 0 else self.got_ref[self.plane(f * ROWS + k)]) for k, t in enumerate(total)]
        index = [[4, 5, 6], [5, 7, 8], [6, 8, 9]]
        values = [score] + [total[1 + c] - y[c] * total[0] for c in range(3)]
        values += [total[index[c][d]] - y[c] * total[1 + d] for c in range(3) for d in range(3)]
        packed = jnp.zeros((blocks, 128), F32)
        for q, value in enumerate(values):
            packed = jnp.where(lane == q, jnp.sum(value, axis=1, keepdims=True), packed)
        flat = jnp.concatenate([packed, jnp.zeros((128 - blocks, 128), F32)], axis=0).T[:16]
        valid = slot_row(self.name_ref, dev, self.place) >= 0
        valid = jnp.concatenate([jnp.where(valid, 1.0, 0.0), jnp.zeros((1, 128 - blocks), F32)], axis=1)
        flat = jnp.where(valid > 0.0, flat, 0.0)
        out = flat[0:4]
        for q in range(1, 4):
            out = out + pltpu.roll(flat[4 * q:4 * q + 4], 32 * q, 1)
        return out

    def chunk(self, dev):
        self.atoms(dev)
        self.templates(dev)
        fronts, middles = {}, {}
        for u in range(self.blocks + 2 * SKEW):
            if u < self.blocks:
                fronts[u] = self.front(u)
            if SKEW <= u < self.blocks + SKEW:
                middles[u - SKEW] = self.middle(*fronts.pop(u - SKEW))
            if u >= 2 * SKEW:
                self.back(*middles.pop(u - 2 * SKEW))
        return self.finish(dev)

    @staticmethod
    def scratch(blocks):
        return [pltpu.VMEM((n * blocks, 128), F32) for n in (48, 6 * ROWS, 3, 8, 24, 5 * ROWS)]


def pair_kernel(me, name_ref, widths_ref, table_ref, real_ref, whole_ref, points_ref, bf_weights_ref, part_ref, out_ref,
                weights_ref, *scratch):
    devices, _, blocks, _ = real_ref.shape
    pairs = Pairs(me(), blocks, name_ref, widths_ref, table_ref, real_ref, whole_ref, points_ref, weights_ref, part_ref, *scratch)
    pairs.clear()

    @pl.loop(0, 5)
    def _(f):
        weights_ref[f] = bf_weights_ref[f].astype(F32)

    @pl.loop(0, devices)
    def _(dev):
        out_ref[dev] = pairs.chunk(dev)


def run_pairs(me, names, widths, table, real, whole, points, weights):
    tmpl_count = points.shape[1]
    devices, _, blocks, _ = real.shape
    vmem = pl.BlockSpec(memory_space=pltpu.VMEM)
    smem = pl.BlockSpec(memory_space=pltpu.SMEM)
    return pl.pallas_call(
        functools.partial(pair_kernel, me),
        out_shape=(jax.ShapeDtypeStruct((5, devices * blocks, 128), F32), jax.ShapeDtypeStruct((devices, 4, 128), F32)),
        in_specs=[vmem, smem, smem, vmem, vmem, vmem, vmem],
        out_specs=(vmem, vmem),
        scratch_shapes=[pltpu.VMEM((5, tmpl_count, 128), F32)] + Pairs.scratch(blocks),
        compiler_params=pltpu.CompilerParams(vmem_limit_bytes=60 << 20),
    )(names, widths, table, real, whole, points, weights)


def return_kernel(libs, tmpls, res_ref, got_ref, local_sem, send_sem, recv_sem):
    l = lax.axis_index("lib")
    t = lax.axis_index("tmpl")
    s = lax.axis_index("sub")
    owners = libs * tmpls
    count = 2 * owners
    me = (l * tmpls + t) * 2 + s
    barrier = pltpu.get_barrier_semaphore()

    def peer(k):
        other = lax.rem(me + k, count)
        return other // 2, {"lib": other // (2 * tmpls), "tmpl": lax.rem(other // 2, tmpls), "sub": lax.rem(other, 2)}

    @pl.loop(1, count)
    def _(k):
        pl.semaphore_signal(barrier, inc=1, device_id=peer(k)[1], device_id_type=MESH)

    local = pltpu.make_async_copy(res_ref.at[l * tmpls + t], got_ref.at[me], local_sem)
    local.start()
    pl.semaphore_wait(barrier, count - 1)

    def copy(k):
        block, where = peer(k)
        return pltpu.make_async_remote_copy(
            src_ref=res_ref.at[block], dst_ref=got_ref.at[me], send_sem=send_sem.at[k], recv_sem=recv_sem.at[k],
            device_id=where, device_id_type=MESH)

    @pl.loop(1, count)
    def _(k):
        copy(k).start()

    local.wait()

    @pl.loop(1, count)
    def _(k):
        copy(k).wait()


def send_back(res, libs, tmpls):
    dma = pltpu.SemaphoreType.DMA
    count = 2 * libs * tmpls
    vmem = pl.BlockSpec(memory_space=pltpu.VMEM)
    return pl.pallas_call(
        functools.partial(return_kernel, libs, tmpls),
        out_shape=jax.ShapeDtypeStruct((count, 4, 128), F32),
        in_specs=[vmem],
        out_specs=vmem,
        scratch_shapes=[dma, dma((count,)), dma((count,))],
        compiler_params=pltpu.CompilerParams(collective_id=1, has_side_effects=True),
    )(res)


def last_kernel(me, got_ref, owner_ref, name_ref, part_ref, score_ref, pose_ref, wg_ref):
    per_block, blocks = owner_ref.shape
    devices = name_ref.shape[0]
    owner = owner_ref[...]
    place = me()

    def add(o, carry):
        total, scores = carry
        both = got_ref[2 * o] + got_ref[2 * o + 1]
        scores = jnp.where(owner == o, jnp.broadcast_to(both[0:1, :blocks], (per_block, blocks)), scores)
        return total + both, scores

    zeros = (jnp.zeros((4, 128), F32), jnp.zeros((per_block, blocks), F32))
    total, scores = lax.fori_loop(0, got_ref.shape[0] // 2, add, zeros)
    score_ref[...] = scores
    rows = [total] + [pltpu.roll(total, 128 - 32 * q, 1) for q in range(1, 4)]
    pose_ref[...] = jnp.concatenate([rows[0][1:4], rows[1], rows[2], rows[3][0:1]], axis=0)[:, :blocks]
    tmpl_count = wg_ref.shape[1]
    step = math.gcd(devices, 8)
    tile = math.gcd(tmpl_count, 256)
    count = step * blocks

    def spread(g):
        rows = []
        for n in range(step):
            row = slot_row(name_ref, g * step + n, place)
            rows.append(row)
        slots = jnp.concatenate(rows, axis=1)
        parts = [part_ref[f, pl.ds(g * count, count)] for f in range(5)]
        halves = [split2(p) for p in parts]
        rhs = jnp.concatenate([jnp.concatenate([h[n] for h in halves], axis=1) for n in range(2)], axis=0)
        for r in range(0, tmpl_count, tile):
            here = lax.broadcasted_iota(jnp.int32, (tile, count), 0) + r
            pick = jnp.where(here == slots, 1.0, 0.0).astype(BF16)
            out = lax.dot_general(jnp.concatenate([pick, pick], axis=1), rhs, (((1,), (0,)), ((), ())), preferred_element_type=F32)
            yield r, out

    for r, out in spread(0):
        for f in range(5):
            wg_ref[f, pl.ds(r, tile)] = out[:, 128 * f:128 * f + 128]

    if devices > step:
        @pl.loop(1, devices // step)
        def _(g):
            for r, out in spread(g):
                for f in range(5):
                    wg_ref[f, pl.ds(r, tile)] += out[:, 128 * f:128 * f + 128]


def last(me, got, owner_rows, names, parts, tmpl_count):
    per_block, blocks = owner_rows.shape
    vmem = pl.BlockSpec(memory_space=pltpu.VMEM)
    return pl.pallas_call(
        functools.partial(last_kernel, me),
        out_shape=(jax.ShapeDtypeStruct((per_block, blocks), F32), jax.ShapeDtypeStruct((12, blocks), F32),
                   jax.ShapeDtypeStruct((5, tmpl_count, 128), F32)),
        in_specs=[vmem] * 4,
        out_specs=(vmem,) * 3,
        compiler_params=pltpu.CompilerParams(vmem_limit_bytes=60 << 20),
    )(got, owner_rows, names, parts)


def local(libs, tmpls, coords, atom_type, channel, charge, pair_owner, pair_slot, type_table, widths, tmpl_points,
          tmpl_weights):
    owners, slots = pair_owner.T, pair_slot.T
    real, whole, names = gather_blocks(jnp.transpose(coords, (1, 0, 2)), charge, atom_type, channel, owners, slots, libs, tmpls)
    count = libs * tmpls
    real, whole, names = [a.reshape((count,) + a.shape[2:]) for a in (real, whole, names)]

    def me():
        return lax.axis_index("lib") * tmpls + lax.axis_index("tmpl")

    parts, res = run_pairs(me, names, widths, type_table.T, real, whole, jnp.transpose(tmpl_points, (1, 0, 2)),
                           jnp.transpose(tmpl_weights, (1, 0, 2)))
    got = send_back(res, libs, tmpls)
    scores, pose, weight_grad = last(me, got, owners, names, parts, tmpl_points.shape[0])
    return scores.T, pose.T, jnp.transpose(weight_grad, (1, 0, 2))


def solution(mesh):
    every = ("groups", "lib", "tmpl")
    in_specs = (P(every, None, None), P(every, None), P(every, None), P(every, None), P(every, None), P(every, None),
                P(), P(), P(("lib", "tmpl"), None, "sub"), P(("lib", "tmpl"), None, "sub"))
    out_specs = (P(every, None), P(every, None), P(every, None, "sub"))
    body = functools.partial(local, mesh.shape["lib"], mesh.shape["tmpl"])
    return jax.shard_map(body, mesh=mesh, in_specs=in_specs, out_specs=out_specs, check_vma=False)
```

time: 52.9 us -> 61.6 us (1.16)
  Pallas kernels: 49.3 us -> 60.7 us
  local copies, waits for them, and re-layouts: 2.53 us -> 0 us
    pallas_call x1, Pallas kernels: 24.2 us -> 32.8 us  [run_pairs(): pl.pallas_call(functools.partial(pair_kernel, me), out_shape=(jax.ShapeDt...]
    pallas_call x1 -> x2, Pallas kernels: 8.1 us -> 10.9 us  [the longest x1 7.98 us: send_back(): pl.pallas_call(functools.partial(return_kernel, libs, tmpls), out_shape=j...]
    unnamed x2 -> x0, local copies, waits for them, and re-layouts: 2.53 us -> none
where the time goes in v1:
time: 61.6 us; the launch traced here: 61.3 us
  Pallas kernels  60.7 us (99%)
  between operations  0.65 us (1%)
    pallas_call x1, Pallas kernels, run_pairs(): pl.pallas_call(functools.partial(pair_kernel, me), out_shape=(jax.ShapeDt...  32.8 us
    pallas_call x1, Pallas kernels, gather_blocks(): pl.pallas_call(functools.partial(gather_kernel, libs, tmpls), out_shape=(...  17 us
    pallas_call x1, Pallas kernels, send_back(): pl.pallas_call(functools.partial(return_kernel, libs, tmpls), out_shape=j...  7.98 us
    pallas_call x1, Pallas kernels, last(): pl.pallas_call(functools.partial(last_kernel, me), out_shape=(jax.ShapeDt...  2.89 us

profile of v1, /device:TPU:0, one launch (start us, length us, event | category | flops | bytes accessed | tf_op | source)
XLA Modules:
  0.0 61.3 jit_solution(2719440988951011439)
XLA Ops:
  0.6 17.0 %shard_map.121 = (f32[4,2,4,32,128]{4,3,2,1,0:T(8,128)}, s32[4,2,2,32,128]{4,3,2,1,0:T(8,128)}, s32[4,2,2,4,32]{4,3,2,1,0:T(4,128)}) custom-call(f32[3,32,128]{2,1,0:T(8,128)} %bitcast.18, f32[32,128]{1,0:T(8,128)} %charge_ref.1, s32[32,128]{1,0:T(8,128)} %type_ref.1, s32[32,128]{1,0:T(8,128)} %chan_ref.1, s32[4,32]{1,0:T(4,128)} %bitcast.19, s32[4,32]{1,0:T(4,128)} %bitcast.21), custom_call_target="tpu_custom_call" | custom-call | tf_op jit(solution)/shard_map/pallas_call | solution.py:122
  17.7 32.8 %shard_map.122 = (f32[5,256,128]{2,1,0:T(8,128)}, f32[8,4,128]{2,1,0:T(4,128)}) custom-call(s32[8,2,4,32]{3,2,1,0:T(4,128)} %bitcast.16, f32[5]{0:T(128)} %widths_ref.1, f32[2,16]{1,0:T(2,128)} %bitcast.22, f32[8,4,32,128]{3,2,1,0:T(8,128)} %bitcast.14, s32[8,2,32,128]{3,2,1,0:T(8,128)} %bitcast.15, f32[3,512,128]{2,1,0:T(8,128)} %bitcast.12, ...), custom_call_target="tpu_custom_call" | custom-call | tf_op jit(solution)/shard_map/pallas_call | solution.py:314
  50.4 8.0 %shard_map.123.got_ref = f32[16,4,128]{2,1,0:T(4,128)} custom-call(f32[8,4,128]{2,1,0:T(4,128)} %get-tuple-element.14.res_ref), custom_call_target="tpu_custom_call" | custom-call | tf_op jit(solution)/shard_map/pallas_call | solution.py:366
  58.4 2.9 %shard_map.124 = (f32[4,32]{1,0:T(4,128)}, f32[12,32]{1,0:T(8,128)}, f32[5,512,128]{2,1,0:T(8,128)}) custom-call(f32[16,4,128]{2,1,0:T(4,128)} %shard_map.123.got_ref, s32[4,32]{1,0:T(4,128)} %bitcast.20, s32[8,2,4,32]{3,2,1,0:T(4,128)} %bitcast.17, f32[5,256,128]{2,1,0:T(8,128)} %get-tuple-element.15.part_ref), custom_call_target="tpu_custom_call" | custom-call | tf_op jit(solution)/shard_map/pallas_call | solution.py:428

commit v2 on v1

v2 whole, which is shorter than its diff:
```python
import functools
import math

import jax
import jax.numpy as jnp
from jax import lax
from jax.experimental import pallas as pl
from jax.experimental.pallas import tpu as pltpu
from jax.sharding import PartitionSpec as P

MESH = pl.DeviceIdType.MESH
F32 = jnp.float32
BF16 = jnp.bfloat16
ROWS = 16
MOMENTS = 10
LEAD = 2
LAG = 1


def split3(a):
    h = a.astype(BF16).astype(F32)
    r = a - h
    m = r.astype(BF16).astype(F32)
    return h, m, r - m


def split2(a):
    h = a.astype(BF16)
    return h, (a - h.astype(F32)).astype(BF16)


def slot_row(name_ref, dev, place):
    named = name_ref[dev, 0] == place
    return jnp.max(jnp.where(named, name_ref[dev, 1], -1), axis=0, keepdims=True)


class Pairs:
    def __init__(self, place, blocks, name_ref, widths_ref, table_ref, real_ref, whole_ref, points_ref, weights_ref, part_ref,
                 atom_ref, moment_ref, rows_ref, tmpl_ref, got_ref):
        self.place, self.blocks = place, blocks
        self.name_ref, self.widths_ref, self.table_ref = name_ref, widths_ref, table_ref
        self.real_ref, self.whole_ref, self.points_ref, self.weights_ref = real_ref, whole_ref, points_ref, weights_ref
        self.part_ref, self.atom_ref, self.moment_ref = part_ref, atom_ref, moment_ref
        self.rows_ref, self.tmpl_ref, self.got_ref = rows_ref, tmpl_ref, got_ref
        self.wide = [widths_ref[f] for f in range(5)]
        log2e = math.log2(math.e)
        self.scale = [-log2e * w for w in self.wide]
        self.ratio = self.wide[1] / self.wide[0]

    def plane(self, n):
        return pl.ds(n * (self.blocks + 1), self.blocks)

    def column(self, n, u, count=8):
        return pl.ds(n * (self.blocks + 1) + u, count, stride=self.blocks + 1)

    def clear(self):
        self.atom_ref[...] = jnp.zeros_like(self.atom_ref)
        self.moment_ref[...] = jnp.zeros_like(self.moment_ref)
        self.tmpl_ref[...] = jnp.zeros_like(self.tmpl_ref)

    def atoms(self, dev):
        x = [self.real_ref[dev, c] for c in range(3)]
        charge = self.real_ref[dev, 3]
        types = self.whole_ref[dev, 0]
        chan = self.whole_ref[dev, 1]
        steric = jnp.zeros(types.shape, F32)
        strength = jnp.zeros(types.shape, F32)
        for n in range(self.table_ref.shape[1]):
            same = types == n
            steric = jnp.where(same, self.table_ref[0, n], steric)
            strength = jnp.where(same, self.table_ref[1, n], strength)
        pharm = jnp.where(chan == 0, self.scale[2], jnp.where(chan == 1, self.scale[3], self.scale[4]))
        second = [x[0] * x[0], x[0] * x[1], x[0] * x[2], x[1] * x[1], x[1] * x[2], x[2] * x[2]]
        norm = second[0] + second[3] + second[5]
        for s, scale in enumerate((self.scale[0], pharm)):
            for c, value in enumerate(x + [norm, None]):
                value = jnp.full(types.shape, scale) if value is None and s == 0 else scale if value is None else value * scale
                for p, piece in enumerate(split3(value)):
                    self.atom_ref[self.plane((3 * s + p) * 8 + c)] = piece
        for c, coef in enumerate((steric, charge, strength)):
            for k, moment in enumerate([None] + x + second):
                value = coef if moment is None else coef * moment
                high = value.astype(BF16).astype(F32)
                low = value - high
                if c < 2:
                    self.moment_ref[self.plane(2 * c * ROWS + k)] = high
                    self.moment_ref[self.plane((2 * c + 1) * ROWS + k)] = low
                    continue
                for n in range(3):
                    self.moment_ref[self.plane(4 * ROWS + n * MOMENTS + k)] = jnp.where(chan == n, high, 0.0)
                    self.moment_ref[self.plane(6 * ROWS + n * MOMENTS + k)] = jnp.where(chan == n, low, 0.0)

    def templates(self, dev):
        slots = jnp.maximum(slot_row(self.name_ref, dev, self.place), 0)
        for u in range(self.blocks):
            there = pl.ds(slots[0, u], 1)
            for c in range(3):
                self.rows_ref[pl.ds(c * (self.blocks + 1) + u, 1)] = self.points_ref[c, there, :]
            for f in range(5):
                self.rows_ref[pl.ds((3 + f) * (self.blocks + 1) + u, 1)] = self.weights_ref[f, there, :]
        y = [self.rows_ref[self.plane(c)] for c in range(3)]
        norm = y[0] * y[0] + y[1] * y[1] + y[2] * y[2]
        for c, value in enumerate([-2.0 * y[0], -2.0 * y[1], -2.0 * y[2], jnp.ones_like(norm), norm]):
            for p, piece in enumerate(split3(value)):
                self.tmpl_ref[self.plane(8 * p + c)] = piece

    def front(self, u):
        def side(ref, base, order):
            pieces = [ref[self.column(base + 8 * p, u)] for p in range(3)]
            return jnp.concatenate([pieces[p] for p in order], axis=0).astype(BF16)

        xs = jnp.concatenate([side(self.atom_ref, 24 * s, (0, 0, 0, 1, 1, 2)) for s in range(2)], axis=1)
        ys = side(self.tmpl_ref, 0, (0, 1, 2, 0, 1, 0))
        return u, lax.dot_general(xs, ys, (((0,), (0,)), ((), ())), preferred_element_type=F32)

    def middle(self, both, e):
        base, rows = ((0, ROWS), (2 * ROWS, ROWS), (4 * ROWS, 2 * ROWS))[e]

        def side(u):
            parts = [self.moment_ref[self.column(base + r, u)] for r in range(0, 2 * rows, 8)]
            return jnp.concatenate(parts, axis=0).astype(BF16)

        powers = [d[128:] if e == 2 else d[:128] * self.ratio if e == 1 else d[:128] for _, d in both]
        lhs = jnp.concatenate([side(u) for u, _ in both], axis=0)
        rhs = jnp.concatenate([jnp.concatenate(split2(jnp.exp2(p)), axis=0) for p in powers], axis=1)
        got = lax.dot_general(jnp.concatenate([lhs, lhs], axis=1), rhs, (((1,), (0,)), ((), ())), preferred_element_type=F32)
        return [u for u, _ in both], base // 2, rows, got

    def back(self, us, base, rows, got):
        for n, u in enumerate(us):
            mine = got[2 * n * rows:(2 * n + 2) * rows, 128 * n:128 * n + 128]
            for r in range(0, rows, 8):
                self.got_ref[self.column(base + r, u)] = mine[r:r + 8] + mine[rows + r:rows + r + 8]

    def got(self, f, k):
        return self.got_ref[self.plane(f * ROWS + k if f < 2 else 2 * ROWS + (f - 2) * MOMENTS + k)]

    def finish(self, dev):
        blocks = self.blocks
        lane = lax.broadcasted_iota(jnp.int32, (blocks, 128), 1)
        y = [self.rows_ref[self.plane(c)] for c in range(3)]
        score = jnp.zeros((blocks, 128), F32)
        total = [jnp.zeros((blocks, 128), F32)] * MOMENTS
        for f in range(5):
            v = self.rows_ref[self.plane(3 + f)]
            first = self.got(f, 0)
            self.part_ref[f, pl.ds(dev * blocks, blocks)] = first
            score = score + v * first
            v = v * (-2.0 * self.wide[f])
            total = [t + v * (first if k == 0 else self.got(f, k)) for k, t in enumerate(total)]
        index = [[4, 5, 6], [5, 7, 8], [6, 8, 9]]
        values = [score] + [total[1 + c] - y[c] * total[0] for c in range(3)]
        values += [total[index[c][d]] - y[c] * total[1 + d] for c in range(3) for d in range(3)]
        packed = jnp.zeros((blocks, 128), F32)
        for q, value in enumerate(values):
            packed = jnp.where(lane == q, jnp.sum(value, axis=1, keepdims=True), packed)
        flat = jnp.concatenate([packed, jnp.zeros((128 - blocks, 128), F32)], axis=0).T[:16]
        valid = slot_row(self.name_ref, dev, self.place) >= 0
        valid = jnp.concatenate([jnp.where(valid, 1.0, 0.0), jnp.zeros((1, 128 - blocks), F32)], axis=1)
        flat = jnp.where(valid > 0.0, flat, 0.0)
        out = flat[0:4]
        for q in range(1, 4):
            out = out + pltpu.roll(flat[4 * q:4 * q + 4], 32 * q, 1)
        return out

    def chunk(self, dev):
        self.atoms(dev)
        self.templates(dev)
        groups = self.blocks // 2
        fronts, middles = {}, {}
        for n in range(3 * groups + LAG):
            g, e = divmod(n, 3)
            for ahead in range(0 if n == 0 else g + LEAD, g + LEAD + 1):
                if e == 0 and ahead < groups:
                    fronts[ahead] = [self.front(2 * ahead), self.front(2 * ahead + 1)]
            if g < groups:
                middles[n] = self.middle(fronts[g], e)
            if n >= LAG:
                self.back(*middles.pop(n - LAG))
        return self.finish(dev)

    @staticmethod
    def scratch(blocks):
        return [pltpu.VMEM((n * (blocks + 1), 128), F32) for n in (48, 8 * ROWS, 8, 24, 4 * ROWS)]


def main_kernel(libs, tmpls, xyz_ref, charge_ref, type_ref, chan_ref, owner_ref, slot_ref, points_hbm, weights_hbm, widths_ref,
                table_ref, part_ref, got_ref, name_ref, real_ref, whole_ref, res_ref, points_ref, bf_ref, weights_ref, local_sem,
                z_send, z_recv, x_send, x_recv, s_send, s_recv, r_send, r_recv, *scratch):
    l = lax.axis_index("lib")
    t = lax.axis_index("tmpl")
    s = lax.axis_index("sub")
    steps = libs * tmpls
    count = 2 * steps
    place = l * tmpls + t
    me = place * 2 + s
    blocks = real_ref.shape[2]
    half = blocks // 2
    moves = [(xyz_ref, real_ref.at[place, pl.ds(0, 3)]), (charge_ref, real_ref.at[place, 3]), (type_ref, whole_ref.at[place, 0]),
             (chan_ref, whole_ref.at[place, 1]), (owner_ref, name_ref.at[place, 0]), (slot_ref, name_ref.at[place, 1]),
             (points_hbm, points_ref), (weights_hbm, bf_ref)]
    moves = [pltpu.make_async_copy(src, dst, local_sem.at[n]) for n, (src, dst) in enumerate(moves)]
    for move in moves:
        move.start()
    barrier = pltpu.get_barrier_semaphore()

    @pl.loop(1, count)
    def _(k):
        other = lax.rem(me + k, count)
        where = {"lib": other // (2 * tmpls), "tmpl": lax.rem(other // 2, tmpls), "sub": lax.rem(other, 2)}
        pl.semaphore_signal(barrier, inc=1, device_id=where, device_id_type=MESH)

    for move in moves[:6]:
        move.wait()
    pl.semaphore_wait(barrier, count - 1)

    def owner_of(k, m):
        return lax.rem(l - k + libs, libs), lax.rem(t - m + tmpls, tmpls)

    def bundle(k, m, send, recv, device):
        lib, tmpl = owner_of(k, m)
        at = lib * tmpls + tmpl
        part = pl.ds(s * half, half)
        refs = (real_ref.at[at, :, part], whole_ref.at[at, :, part], name_ref.at[at, s])
        return [pltpu.make_async_remote_copy(src_ref=ref, dst_ref=ref, send_sem=send(n), recv_sem=recv(n), device_id=device,
                                             device_id_type=MESH) for n, ref in enumerate(refs)]

    def z_copy(k):
        return bundle(0, 0, lambda n: z_send.at[k, n], lambda n: z_recv.at[k, n], {"lib": lax.rem(l + k, libs)})

    def x_copy(k, m):
        return bundle(k, 0, lambda n: x_send.at[k, m, n], lambda n: x_recv.at[k, m, n], {"tmpl": lax.rem(t + m, tmpls)})

    def s_copy(k, m):
        return bundle(k, m, lambda n: s_send.at[k, m, n], lambda n: s_recv.at[k, m, n], {"sub": 1 - s})

    def back_copy(i, c):
        lib, tmpl = owner_of(i // tmpls, lax.rem(i, tmpls))
        where = {"lib": lib, "tmpl": tmpl, "sub": 1 - s} if c else {"lib": lib, "tmpl": tmpl}
        return pltpu.make_async_remote_copy(
            src_ref=res_ref.at[lib * tmpls + tmpl], dst_ref=got_ref.at[me], send_sem=r_send.at[i, c],
            recv_sem=r_recv.at[i, c], device_id=where, device_id_type=MESH)

    def all_of(copies, act):
        for c in copies:
            getattr(c, act)()

    def z_pump(k):
        all_of(z_copy(k), "wait_recv")

        @pl.loop(1, tmpls)
        def _(m):
            all_of(x_copy(k, m), "start")

        all_of(s_copy(k, 0), "start")

    def x_pump(k, m):
        all_of(x_copy(k, m), "wait_recv")
        all_of(s_copy(k, m), "start")

    @pl.loop(1, tmpls)
    def _(m):
        all_of(x_copy(0, m), "start")

    @pl.loop(1, libs)
    def _(k):
        all_of(z_copy(k), "start")

    pairs = Pairs(place, blocks, name_ref, widths_ref, table_ref, real_ref, whole_ref, points_ref, weights_ref, part_ref, *scratch)
    pairs.clear()
    for move in moves[6:]:
        move.wait()

    @pl.loop(0, 5)
    def _(f):
        weights_ref[f] = bf_ref[f].astype(F32)

    mine = pltpu.make_async_copy(res_ref.at[place], got_ref.at[me], local_sem.at[8])

    @pl.loop(0, steps)
    def _(i):
        k = i // tmpls
        m = lax.rem(i, tmpls)

        @pl.when((i > 0) & (m == 0) & (k + 1 < libs))
        def _():
            z_pump(k + 1)

        @pl.when((i > 0) & (m + 1 < tmpls))
        def _():
            x_pump(k, m + 1)

        @pl.when(i > 0)
        def _():
            all_of(s_copy(k, m), "wait_recv")

        @pl.when(i == 1)
        def _():
            mine.start()

        @pl.when(i > 0)
        def _():
            back_copy(i - 1, 1).start()

        @pl.when(i > 1)
        def _():
            back_copy(i - 1, 0).start()

        lib, tmpl = owner_of(k, m)
        dev = lib * tmpls + tmpl
        res_ref[dev] = pairs.chunk(dev)

        @pl.when(i == 0)
        def _():
            if tmpls > 1:
                x_pump(0, 1)
            if libs > 1:
                z_pump(1)

    mine.wait()

    @pl.loop(1, libs)
    def _(k):
        all_of(z_copy(k), "wait_send")
        all_of(s_copy(k, 0), "wait_send")

    @pl.loop(1, tmpls)
    def _(m):
        @pl.loop(0, libs)
        def _(k):
            all_of(x_copy(k, m), "wait_send")
            all_of(s_copy(k, m), "wait_send")

    back_copy(steps - 1, 1).start()
    back_copy(steps - 1, 0).start()
    back_copy(0, 1).wait()

    @pl.loop(1, steps)
    def _(i):
        for c in range(2):
            back_copy(i, c).wait()


def run(libs, tmpls, xyz, charge, types, chans, owners, slots, points, weights, widths, table):
    blocks = charge.shape[0]
    steps = libs * tmpls
    dma = pltpu.SemaphoreType.DMA
    vmem = pl.BlockSpec(memory_space=pltpu.VMEM)
    smem = pl.BlockSpec(memory_space=pltpu.SMEM)
    lead = (libs, tmpls)
    return pl.pallas_call(
        functools.partial(main_kernel, libs, tmpls),
        out_shape=(jax.ShapeDtypeStruct((5, steps * blocks, 128), F32), jax.ShapeDtypeStruct((2 * steps, 4, 128), F32),
                   jax.ShapeDtypeStruct((steps, 2) + owners.shape, jnp.int32)),
        in_specs=[pl.BlockSpec(memory_space=pl.ANY)] * 8 + [smem, smem],
        out_specs=(vmem,) * 3,
        scratch_shapes=[pltpu.VMEM((steps, 4, blocks, 128), F32), pltpu.VMEM((steps, 2, blocks, 128), jnp.int32),
                        pltpu.VMEM((steps, 4, 128), F32), pltpu.VMEM(points.shape, F32), pltpu.VMEM(weights.shape, BF16),
                        pltpu.VMEM(weights.shape, F32), dma((9,)), dma((libs, 3)), dma((libs, 3)), dma(lead + (3,)),
                        dma(lead + (3,)), dma(lead + (3,)), dma(lead + (3,)), dma((steps, 2)), dma((steps, 2))]
        + Pairs.scratch(blocks),
        compiler_params=pltpu.CompilerParams(collective_id=0, has_side_effects=True, vmem_limit_bytes=60 << 20),
    )(xyz, charge, types, chans, owners, slots, points, weights, widths, table)


def last_kernel(me, got_ref, owner_ref, name_ref, part_ref, score_ref, pose_ref, wg_ref):
    per_block, blocks = owner_ref.shape
    devices = name_ref.shape[0]
    owner = owner_ref[...]
    place = me()

    def add(o, carry):
        total, scores = carry
        both = got_ref[2 * o] + got_ref[2 * o + 1]
        scores = jnp.where(owner == o, jnp.broadcast_to(both[0:1, :blocks], (per_block, blocks)), scores)
        return total + both, scores

    zeros = (jnp.zeros((4, 128), F32), jnp.zeros((per_block, blocks), F32))
    total, scores = lax.fori_loop(0, got_ref.shape[0] // 2, add, zeros)
    score_ref[...] = scores
    rows = [total] + [pltpu.roll(total, 128 - 32 * q, 1) for q in range(1, 4)]
    pose_ref[...] = jnp.concatenate([rows[0][1:4], rows[1], rows[2], rows[3][0:1]], axis=0)[:, :blocks]
    tmpl_count = wg_ref.shape[1]
    step = math.gcd(devices, 8)
    tile = math.gcd(tmpl_count, 256)
    count = step * blocks

    def spread(g):
        rows = []
        for n in range(step):
            row = slot_row(name_ref, g * step + n, place)
            rows.append(row)
        slots = jnp.concatenate(rows, axis=1)
        parts = [part_ref[f, pl.ds(g * count, count)] for f in range(5)]
        halves = [split2(p) for p in parts]
        rhs = jnp.concatenate([jnp.concatenate([h[n] for h in halves], axis=1) for n in range(2)], axis=0)
        for r in range(0, tmpl_count, tile):
            here = lax.broadcasted_iota(jnp.int32, (tile, count), 0) + r
            pick = jnp.where(here == slots, 1.0, 0.0).astype(BF16)
            out = lax.dot_general(jnp.concatenate([pick, pick], axis=1), rhs, (((1,), (0,)), ((), ())), preferred_element_type=F32)
            yield r, out

    for r, out in spread(0):
        for f in range(5):
            wg_ref[f, pl.ds(r, tile)] = out[:, 128 * f:128 * f + 128]

    if devices > step:
        @pl.loop(1, devices // step)
        def _(g):
            for r, out in spread(g):
                for f in range(5):
                    wg_ref[f, pl.ds(r, tile)] += out[:, 128 * f:128 * f + 128]


def last(me, got, owner_rows, names, parts, tmpl_count):
    per_block, blocks = owner_rows.shape
    vmem = pl.BlockSpec(memory_space=pltpu.VMEM)
    return pl.pallas_call(
        functools.partial(last_kernel, me),
        out_shape=(jax.ShapeDtypeStruct((per_block, blocks), F32), jax.ShapeDtypeStruct((12, blocks), F32),
                   jax.ShapeDtypeStruct((5, tmpl_count, 128), F32)),
        in_specs=[vmem] * 4,
        out_specs=(vmem,) * 3,
        compiler_params=pltpu.CompilerParams(vmem_limit_bytes=60 << 20),
    )(got, owner_rows, names, parts)


def local(libs, tmpls, coords, atom_type, channel, charge, pair_owner, pair_slot, type_table, widths, tmpl_points,
          tmpl_weights):
    owners, slots = pair_owner.T, pair_slot.T

    def me():
        return lax.axis_index("lib") * tmpls + lax.axis_index("tmpl")

    parts, got, names = run(libs, tmpls, jnp.transpose(coords, (1, 0, 2)), charge, atom_type, channel, owners, slots,
                            jnp.transpose(tmpl_points, (1, 0, 2)), jnp.transpose(tmpl_weights, (1, 0, 2)), widths, type_table.T)
    scores, pose, weight_grad = last(me, got, owners, names, parts, tmpl_points.shape[0])
    return scores.T, pose.T, jnp.transpose(weight_grad, (1, 0, 2))


def solution(mesh):
    every = ("groups", "lib", "tmpl")
    in_specs = (P(every, None, None), P(every, None), P(every, None), P(every, None), P(every, None), P(every, None),
                P(), P(), P(("lib", "tmpl"), None, "sub"), P(("lib", "tmpl"), None, "sub"))
    out_specs = (P(every, None), P(every, None), P(every, None, "sub"))
    body = functools.partial(local, mesh.shape["lib"], mesh.shape["tmpl"])
    return jax.shard_map(body, mesh=mesh, in_specs=in_specs, out_specs=out_specs, check_vma=False)
```

time: 61.6 us -> 37.8 us (0.61)
  Pallas kernels: 60.7 us -> 36.9 us
    pallas_call x3 -> x1, Pallas kernels: 57.8 us -> 34 us  [run(): pl.pallas_call(functools.partial(main_kernel, libs, tmpls), out_shape=(ja...]
where the time goes in v2:
time: 37.8 us; the launch traced here: 37.6 us
  Pallas kernels  36.9 us (98%)
  between operations  0.64 us (2%)
    pallas_call x1, Pallas kernels, run(): pl.pallas_call(functools.partial(main_kernel, libs, tmpls), out_shape=(ja...  34 us
    pallas_call x1, Pallas kernels, last(): pl.pallas_call(functools.partial(last_kernel, me), out_shape=(jax.ShapeDt...  2.9 us

profile of v2, /device:TPU:0, one launch (start us, length us, event | category | flops | bytes accessed | tf_op | source)
XLA Modules:
  0.0 37.6 jit_solution(1605926691525275265)
XLA Ops:
  0.6 34.0 %shard_map.121 = (f32[5,256,128]{2,1,0:T(8,128)}, f32[16,4,128]{2,1,0:T(4,128)}, s32[8,2,4,32]{3,2,1,0:T(4,128)}) custom-call(f32[3,32,128]{2,1,0:T(8,128)} %bitcast.11, f32[32,128]{1,0:T(8,128)} %charge_ref.1, s32[32,128]{1,0:T(8,128)} %type_ref.1, s32[32,128]{1,0:T(8,128)} %chan_ref.1, s32[4,32]{1,0:T(4,128)} %bitcast.12, s32[4,32]{1,0:T(4,128)} %bitcast.14, ...), custom_call_target="tpu_custom_call" | custom-call | tf_op jit(solution)/shard_map/pallas_call | solution.py:351
  34.7 2.9 %shard_map.122 = (f32[4,32]{1,0:T(4,128)}, f32[12,32]{1,0:T(8,128)}, f32[5,512,128]{2,1,0:T(8,128)}) custom-call(f32[16,4,128]{2,1,0:T(4,128)} %get-tuple-element.9.got_ref, s32[4,32]{1,0:T(4,128)} %bitcast.13, s32[8,2,4,32]{3,2,1,0:T(4,128)} %get-tuple-element.10.name_ref, f32[5,256,128]{2,1,0:T(8,128)} %get-tuple-element.11.part_ref), custom_call_target="tpu_custom_call" | custom-call | tf_op jit(solution)/shard_map/pallas_call | solution.py:418

commit v3 on v2

--- a/solution.py
+++ b/solution.py
@@ -13,7 +13,7 @@
 BF16 = jnp.bfloat16
 ROWS = 16
 MOMENTS = 10
-LEAD = 2
+LEAD = 10
 LAG = 1
 
 
@@ -113,24 +113,18 @@
         ys = side(self.tmpl_ref, 0, (0, 1, 2, 0, 1, 0))
         return u, lax.dot_general(xs, ys, (((0,), (0,)), ((), ())), preferred_element_type=F32)
 
-    def middle(self, both, e):
+    def middle(self, u, dist, e):
         base, rows = ((0, ROWS), (2 * ROWS, ROWS), (4 * ROWS, 2 * ROWS))[e]
-
-        def side(u):
-            parts = [self.moment_ref[self.column(base + r, u)] for r in range(0, 2 * rows, 8)]
-            return jnp.concatenate(parts, axis=0).astype(BF16)
-
-        powers = [d[128:] if e == 2 else d[:128] * self.ratio if e == 1 else d[:128] for _, d in both]
-        lhs = jnp.concatenate([side(u) for u, _ in both], axis=0)
-        rhs = jnp.concatenate([jnp.concatenate(split2(jnp.exp2(p)), axis=0) for p in powers], axis=1)
-        got = lax.dot_general(jnp.concatenate([lhs, lhs], axis=1), rhs, (((1,), (0,)), ((), ())), preferred_element_type=F32)
-        return [u for u, _ in both], base // 2, rows, got
-
-    def back(self, us, base, rows, got):
-        for n, u in enumerate(us):
-            mine = got[2 * n * rows:(2 * n + 2) * rows, 128 * n:128 * n + 128]
-            for r in range(0, rows, 8):
-                self.got_ref[self.column(base + r, u)] = mine[r:r + 8] + mine[rows + r:rows + r + 8]
+        power = dist[128:] if e == 2 else dist[:128] * self.ratio if e == 1 else dist[:128]
+        lhs = jnp.concatenate([self.moment_ref[self.column(base + r, u)] for r in range(0, 2 * rows, 8)], axis=0).astype(BF16)
+        rhs = jnp.concatenate(split2(jnp.exp2(power)), axis=1)
+        got = lax.dot_general(lhs, rhs, (((1,), (0,)), ((), ())), preferred_element_type=F32)
+        return u, base // 2, rows, got
+
+    def back(self, u, base, rows, got):
+        for r in range(0, rows, 8):
+            mine = got[r:r + 8, :128] + got[r:r + 8, 128:] + got[rows + r:rows + r + 8, :128]
+            self.got_ref[self.column(base + r, u)] = mine
 
     def got(self, f, k):
         return self.got_ref[self.plane(f * ROWS + k if f < 2 else 2 * ROWS + (f - 2) * MOMENTS + k)]
@@ -166,15 +160,14 @@
     def chunk(self, dev):
         self.atoms(dev)
         self.templates(dev)
-        groups = self.blocks // 2
         fronts, middles = {}, {}
-        for n in range(3 * groups + LAG):
-            g, e = divmod(n, 3)
-            for ahead in range(0 if n == 0 else g + LEAD, g + LEAD + 1):
-                if e == 0 and ahead < groups:
-                    fronts[ahead] = [self.front(2 * ahead), self.front(2 * ahead + 1)]
-            if g < groups:
-                middles[n] = self.middle(fronts[g], e)
+        for n in range(-LEAD, 3 * self.blocks + LAG):
+            u, e = divmod(n + LEAD, 3)
+            if e == 0 and 0 <= u < self.blocks:
+                fronts[u] = self.front(u)[1]
+            u, e = divmod(n, 3)
+            if 0 <= u < self.blocks:
+                middles[n] = self.middle(u, fronts[u], e)
             if n >= LAG:
                 self.back(*middles.pop(n - LAG))
         return self.finish(dev)
@@ -214,8 +207,22 @@
         move.wait()
     pl.semaphore_wait(barrier, count - 1)
 
+    def lib_of(k, sign):
+        if libs & (libs - 1):
+            return lax.rem(l + sign * k + libs, libs)
+        bits = [1 << b for b in range(libs.bit_length() - 1)]
+        return sum((lax.rem(l // bit + k // bit, 2) * bit for bit in bits), jnp.int32(0))
+
     def owner_of(k, m):
-        return lax.rem(l - k + libs, libs), lax.rem(t - m + tmpls, tmpls)
+        return lib_of(k, -1), lax.rem(t - m + tmpls, tmpls)
+
+    def step_of(i):
+        j = i // tmpls
+        m = lax.rem(i, tmpls)
+        return lib_step(j), m + ((j + 1) // libs) * (tmpls - 1 - 2 * m)
+
+    def lib_step(j):
+        return (lax.rem(j, max(libs - 1, 1)) + 1) * ((j + libs - 1) // libs)
 
     def bundle(k, m, send, recv, device):
         lib, tmpl = owner_of(k, m)
@@ -226,7 +233,7 @@
                                              device_id_type=MESH) for n, ref in enumerate(refs)]
 
     def z_copy(k):
-        return bundle(0, 0, lambda n: z_send.at[k, n], lambda n: z_recv.at[k, n], {"lib": lax.rem(l + k, libs)})
+        return bundle(0, 0, lambda n: z_send.at[k, n], lambda n: z_recv.at[k, n], {"lib": lib_of(k, 1)})
 
     def x_copy(k, m):
         return bundle(k, 0, lambda n: x_send.at[k, m, n], lambda n: x_recv.at[k, m, n], {"tmpl": lax.rem(t + m, tmpls)})
@@ -235,7 +242,7 @@
         return bundle(k, m, lambda n: s_send.at[k, m, n], lambda n: s_recv.at[k, m, n], {"sub": 1 - s})
 
     def back_copy(i, c):
-        lib, tmpl = owner_of(i // tmpls, lax.rem(i, tmpls))
+        lib, tmpl = owner_of(*step_of(i))
         where = {"lib": lib, "tmpl": tmpl, "sub": 1 - s} if c else {"lib": lib, "tmpl": tmpl}
         return pltpu.make_async_remote_copy(
             src_ref=res_ref.at[lib * tmpls + tmpl], dst_ref=got_ref.at[me], send_sem=r_send.at[i, c],
@@ -263,8 +270,8 @@
         all_of(x_copy(0, m), "start")
 
     @pl.loop(1, libs)
-    def _(k):
-        all_of(z_copy(k), "start")
+    def _(j):
+        all_of(z_copy(lib_step(j)), "start")
 
     pairs = Pairs(place, blocks, name_ref, widths_ref, table_ref, real_ref, whole_ref, points_ref, weights_ref, part_ref, *scratch)
     pairs.clear()
@@ -279,16 +286,17 @@
 
     @pl.loop(0, steps)
     def _(i):
-        k = i // tmpls
-        m = lax.rem(i, tmpls)
-
-        @pl.when((i > 0) & (m == 0) & (k + 1 < libs))
-        def _():
-            z_pump(k + 1)
-
-        @pl.when((i > 0) & (m + 1 < tmpls))
-        def _():
-            x_pump(k, m + 1)
+        k, m = step_of(i)
+        j = i // tmpls
+        k1, m1 = step_of(i + 1)
+
+        @pl.when((i > 0) & (lax.rem(i, tmpls) == 0) & (j + 1 < libs))
+        def _():
+            z_pump(lib_step(j + 1))
+
+        @pl.when((i > 0) & (i + 1 < steps) & (m1 > 0))
+        def _():
+            x_pump(k1, m1)
 
         @pl.when(i > 0)
         def _():
@@ -315,7 +323,7 @@
             if tmpls > 1:
                 x_pump(0, 1)
             if libs > 1:
-                z_pump(1)
+                z_pump(lib_step(1))
 
     mine.wait()
 

time: 37.8 us -> 37.1 us (0.981)
  Pallas kernels: 36.9 us -> 36.2 us
    pallas_call x1, Pallas kernels: 34 us -> 33.3 us  [run(): pl.pallas_call(functools.partial(main_kernel, libs, tmpls), out_shape=(ja...]
where the time goes in v3:
time: 37.1 us; the launch traced here: 36.9 us
  Pallas kernels  36.2 us (98%)
  between operations  0.64 us (2%)
    pallas_call x1, Pallas kernels, run(): pl.pallas_call(functools.partial(main_kernel, libs, tmpls), out_shape=(ja...  33.3 us
    pallas_call x1, Pallas kernels, last(): pl.pallas_call(functools.partial(last_kernel, me), out_shape=(jax.ShapeDt...  2.89 us

profile of v3, /device:TPU:0, one launch (start us, length us, event | category | flops | bytes accessed | tf_op | source)
XLA Modules:
  0.0 36.9 jit_solution(9842819669960568529)
XLA Ops:
  0.6 33.3 %shard_map.121 = (f32[5,256,128]{2,1,0:T(8,128)}, f32[16,4,128]{2,1,0:T(4,128)}, s32[8,2,4,32]{3,2,1,0:T(4,128)}) custom-call(f32[3,32,128]{2,1,0:T(8,128)} %bitcast.11, f32[32,128]{1,0:T(8,128)} %charge_ref.1, s32[32,128]{1,0:T(8,128)} %type_ref.1, s32[32,128]{1,0:T(8,128)} %chan_ref.1, s32[4,32]{1,0:T(4,128)} %bitcast.12, s32[4,32]{1,0:T(4,128)} %bitcast.14, ...), custom_call_target="tpu_custom_call" | custom-call | tf_op jit(solution)/shard_map/pallas_call | solution.py:359
  34.0 2.9 %shard_map.122 = (f32[4,32]{1,0:T(4,128)}, f32[12,32]{1,0:T(8,128)}, f32[5,512,128]{2,1,0:T(8,128)}) custom-call(f32[16,4,128]{2,1,0:T(4,128)} %get-tuple-element.9.got_ref, s32[4,32]{1,0:T(4,128)} %bitcast.13, s32[8,2,4,32]{3,2,1,0:T(4,128)} %get-tuple-element.10.name_ref, f32[5,256,128]{2,1,0:T(8,128)} %get-tuple-element.11.part_ref), custom_call_target="tpu_custom_call" | custom-call | tf_op jit(solution)/shard_map/pallas_call | solution.py:426

commit v4 on v3

--- a/solution.py
+++ b/solution.py
@@ -177,8 +177,9 @@
         return [pltpu.VMEM((n * (blocks + 1), 128), F32) for n in (48, 8 * ROWS, 8, 24, 4 * ROWS)]
 
 
-def main_kernel(libs, tmpls, xyz_ref, charge_ref, type_ref, chan_ref, owner_ref, slot_ref, points_hbm, weights_hbm, widths_ref,
-                table_ref, part_ref, got_ref, name_ref, real_ref, whole_ref, res_ref, points_ref, bf_ref, weights_ref, local_sem,
+def main_kernel(libs, tmpls, xyz_ref, charge_ref, type_ref, chan_ref, owner_ref, slot_ref, points_hbm, weights_hbm, widths_hbm,
+                table_hbm, part_hbm, got_ref, name_ref, real_ref, whole_ref, res_ref, points_ref, bf_ref, weights_ref, widths_ref, table_ref,
+                part_ref, part_sem, local_sem,
                 z_send, z_recv, x_send, x_recv, s_send, s_recv, r_send, r_recv, *scratch):
     l = lax.axis_index("lib")
     t = lax.axis_index("tmpl")
@@ -191,7 +192,7 @@
     half = blocks // 2
     moves = [(xyz_ref, real_ref.at[place, pl.ds(0, 3)]), (charge_ref, real_ref.at[place, 3]), (type_ref, whole_ref.at[place, 0]),
              (chan_ref, whole_ref.at[place, 1]), (owner_ref, name_ref.at[place, 0]), (slot_ref, name_ref.at[place, 1]),
-             (points_hbm, points_ref), (weights_hbm, bf_ref)]
+             (widths_hbm, widths_ref), (table_hbm, table_ref), (points_hbm, points_ref), (weights_hbm, bf_ref)]
     moves = [pltpu.make_async_copy(src, dst, local_sem.at[n]) for n, (src, dst) in enumerate(moves)]
     for move in moves:
         move.start()
@@ -222,7 +223,7 @@
         return lib_step(j), m + ((j + 1) // libs) * (tmpls - 1 - 2 * m)
 
     def lib_step(j):
-        return (lax.rem(j, max(libs - 1, 1)) + 1) * ((j + libs - 1) // libs)
+        return (lax.rem((2 - libs % 2) * (j + libs - 2), max(libs - 1, 1)) + 1) * ((j + libs - 1) // libs)
 
     def bundle(k, m, send, recv, device):
         lib, tmpl = owner_of(k, m)
@@ -248,6 +249,11 @@
             src_ref=res_ref.at[lib * tmpls + tmpl], dst_ref=got_ref.at[me], send_sem=r_send.at[i, c],
             recv_sem=r_recv.at[i, c], device_id=where, device_id_type=MESH)
 
+    def part_copy(i):
+        lib, tmpl = owner_of(*step_of(i))
+        here = pl.ds((lib * tmpls + tmpl) * blocks, blocks)
+        return pltpu.make_async_copy(part_ref.at[:, here], part_hbm.at[:, here], part_sem.at[i])
+
     def all_of(copies, act):
         for c in copies:
             getattr(c, act)()
@@ -273,16 +279,17 @@
     def _(j):
         all_of(z_copy(lib_step(j)), "start")
 
+    for move in moves[6:]:
+        move.wait()
+
     pairs = Pairs(place, blocks, name_ref, widths_ref, table_ref, real_ref, whole_ref, points_ref, weights_ref, part_ref, *scratch)
     pairs.clear()
-    for move in moves[6:]:
-        move.wait()
 
     @pl.loop(0, 5)
     def _(f):
         weights_ref[f] = bf_ref[f].astype(F32)
 
-    mine = pltpu.make_async_copy(res_ref.at[place], got_ref.at[me], local_sem.at[8])
+    mine = pltpu.make_async_copy(res_ref.at[place], got_ref.at[me], local_sem.at[10])
 
     @pl.loop(0, steps)
     def _(i):
@@ -309,6 +316,7 @@
         @pl.when(i > 0)
         def _():
             back_copy(i - 1, 1).start()
+            part_copy(i - 1).start()
 
         @pl.when(i > 1)
         def _():
@@ -341,7 +349,12 @@
 
     back_copy(steps - 1, 1).start()
     back_copy(steps - 1, 0).start()
+    part_copy(steps - 1).start()
     back_copy(0, 1).wait()
+
+    @pl.loop(0, steps)
+    def _(i):
+        part_copy(i).wait()
 
     @pl.loop(1, steps)
     def _(i):
@@ -354,17 +367,17 @@
     steps = libs * tmpls
     dma = pltpu.SemaphoreType.DMA
     vmem = pl.BlockSpec(memory_space=pltpu.VMEM)
-    smem = pl.BlockSpec(memory_space=pltpu.SMEM)
     lead = (libs, tmpls)
     return pl.pallas_call(
         functools.partial(main_kernel, libs, tmpls),
         out_shape=(jax.ShapeDtypeStruct((5, steps * blocks, 128), F32), jax.ShapeDtypeStruct((2 * steps, 4, 128), F32),
                    jax.ShapeDtypeStruct((steps, 2) + owners.shape, jnp.int32)),
-        in_specs=[pl.BlockSpec(memory_space=pl.ANY)] * 8 + [smem, smem],
-        out_specs=(vmem,) * 3,
+        in_specs=[pl.BlockSpec(memory_space=pl.ANY)] * 10,
+        out_specs=(pl.BlockSpec(memory_space=pl.ANY), vmem, vmem),
         scratch_shapes=[pltpu.VMEM((steps, 4, blocks, 128), F32), pltpu.VMEM((steps, 2, blocks, 128), jnp.int32),
                         pltpu.VMEM((steps, 4, 128), F32), pltpu.VMEM(points.shape, F32), pltpu.VMEM(weights.shape, BF16),
-                        pltpu.VMEM(weights.shape, F32), dma((9,)), dma((libs, 3)), dma((libs, 3)), dma(lead + (3,)),
+                        pltpu.VMEM(weights.shape, F32), pltpu.SMEM(widths.shape, F32), pltpu.SMEM(table.shape, F32),
+                        pltpu.VMEM((5, steps * blocks, 128), F32), dma((steps,)), dma((11,)), dma((libs, 3)), dma((libs, 3)), dma(lead + (3,)),
                         dma(lead + (3,)), dma(lead + (3,)), dma(lead + (3,)), dma((steps, 2)), dma((steps, 2))]
         + Pairs.scratch(blocks),
         compiler_params=pltpu.CompilerParams(collective_id=0, has_side_effects=True, vmem_limit_bytes=60 << 20),

time: 37.1 us -> 35.5 us (0.957)
  Pallas kernels: 36.2 us -> 34.7 us
    pallas_call x1, Pallas kernels: 33.3 us -> 31.8 us  [run(): pl.pallas_call(functools.partial(main_kernel, libs, tmpls), out_shape=(ja...]
where the time goes in v4:
time: 35.5 us; the launch traced here: 35.3 us
  Pallas kernels  34.7 us (98%)
  between operations  0.64 us (2%)
    pallas_call x1, Pallas kernels, run(): pl.pallas_call(functools.partial(main_kernel, libs, tmpls), out_shape=(ja...  31.8 us
    pallas_call x1, Pallas kernels, last(): pl.pallas_call(functools.partial(last_kernel, me), out_shape=(jax.ShapeDt...  2.89 us

profile of v4, /device:TPU:0, one launch (start us, length us, event | category | flops | bytes accessed | tf_op | source)
XLA Modules:
  0.0 35.3 jit_solution(18063488951275188189)
XLA Ops:
  0.6 31.8 %shard_map.121 = (f32[5,256,128]{2,1,0:T(8,128)}, f32[16,4,128]{2,1,0:T(4,128)}, s32[8,2,4,32]{3,2,1,0:T(4,128)}) custom-call(f32[3,32,128]{2,1,0:T(8,128)} %bitcast.11, f32[32,128]{1,0:T(8,128)} %charge_ref.1, s32[32,128]{1,0:T(8,128)} %type_ref.1, s32[32,128]{1,0:T(8,128)} %chan_ref.1, s32[4,32]{1,0:T(4,128)} %bitcast.12, s32[4,32]{1,0:T(4,128)} %bitcast.14, ...), custom_call_target="tpu_custom_call" | custom-call | tf_op jit(solution)/shard_map/pallas_call | solution.py:371
  32.5 2.9 %shard_map.122 = (f32[4,32]{1,0:T(4,128)}, f32[12,32]{1,0:T(8,128)}, f32[5,512,128]{2,1,0:T(8,128)}) custom-call(f32[16,4,128]{2,1,0:T(4,128)} %get-tuple-element.9.got_ref, s32[4,32]{1,0:T(4,128)} %bitcast.13, s32[8,2,4,32]{3,2,1,0:T(4,128)} %get-tuple-element.10.name_ref, f32[5,256,128]{2,1,0:T(8,128)} %get-tuple-element.11.part_ref), custom_call_target="tpu_custom_call" | custom-call | tf_op jit(solution)/shard_map/pallas_call | solution.py:439
